TPU v7x, 512 devices: a whole 4x8x8 slice. The times are simulated.
512 devices in a mesh: dp: 64 (over y, x, core), tensor: 8 (over z).
Axes of the slice: x: 4, y: 8, z: 8, core: 2. Of those that a mesh axis runs over, the one named last changes fastest.
Arguments:
- hidden_act: bfloat16 [32768, 1408], P('dp', 'tensor'), may hold values from -6 to 6
- cotangent: bfloat16 [32768, 2048], P('dp', 'tensor'), may hold values from -4 to 4
- down_table: bfloat16 [1408, 64, 2048], P('tensor', 'dp'), may hold values from -0.15625 to 0.15625
- expert_ids: int32 [128, 4], P('dp'), may hold values from 0 to 31, as said below
- merge_weights: float32 [128, 4], P('dp'), may hold values from 0.1 to 1
- owner_slot: int32 [32], replicated, may hold values from 0 to 63, as said below
Outputs:
- layer_out: bfloat16 [32768, 2048], P('dp', 'tensor')
- grad_hidden: bfloat16 [32768, 1408], P('dp', 'tensor')
- expert_grad: float32 [1408, 64, 2048], P('tensor', 'dp')
Inputs may be any that keep to these rules, and one draw needn't show every extreme that they name: `expert_ids`: each segment lists 4 different experts; the 2 segments of one index of dp list exactly 6 different experts together. `owner_slot`: different experts have different slots; slot 63 always holds an expert.
All inputs are finite; a program needn't handle non-finite values.
Results may differ from a plain program's by a relative error of at most 0.013.
Values may be sent and summed in bfloat16 or wider, within the bound.
A program may use at most 128 MiB of HBM per device.

v0:
```python
import jax
import jax.numpy as jnp
from jax import lax
from jax.sharding import PartitionSpec as P

E = 32
K = 4
POOL = 6


def pool_members(id_rows):
    listed = id_rows.reshape(-1)
    experts = jnp.arange(E, dtype=jnp.int32)
    present = jnp.any(listed[None, :] == experts[:, None], axis=1)
    ranking = jnp.cumsum(present.astype(jnp.int32)) - 1
    places = jnp.arange(POOL, dtype=jnp.int32)
    chosen = present[None, :] & (ranking[None, :] == places[:, None])
    return jnp.sum(jnp.where(chosen, experts[None, :], 0), axis=1)


def merge_coefficients(id_rows, weight_rows, targets):
    matches = id_rows[:, :, None] == targets[None, None, :]
    return jnp.sum(jnp.where(matches, weight_rows[:, :, None], 0.0), axis=1)


def body(hidden_act, cotangent, down_table, expert_ids, merge_weights, owner_slot):
    dp_count = lax.axis_size("dp")
    seg_count = expert_ids.shape[0]
    ff_local, slot_local, width = down_table.shape
    stripe = width // dp_count
    row_count = hidden_act.shape[0]
    seg_len = row_count // seg_count
    every_expert = jnp.arange(E, dtype=jnp.int32)
    all_ids, all_weights = (
        lax.all_gather(expert_ids, "dp", axis=0, tiled=True),
        lax.all_gather(merge_weights, "dp", axis=0, tiled=True),
    )
    ids_by_dev = all_ids.reshape(dp_count, seg_count, K)
    weights_by_dev = all_weights.reshape(dp_count, seg_count, K)
    pools_all = jax.vmap(pool_members)(ids_by_dev)
    my_pool = pools_all[lax.axis_index("dp")]
    my_coef = merge_coefficients(expert_ids, merge_weights, my_pool)
    member_table = (pools_all.T[:, :, None] == every_expert[None, None, :]).astype(jnp.bfloat16)
    stripes = lax.all_to_all(down_table, "dp", split_axis=2, concat_axis=1, tiled=True)
    by_expert = jnp.take(stripes, owner_slot, axis=1)
    outgoing = jnp.take(by_expert, pools_all.T, axis=1).reshape(ff_local, POOL, width)
    panel_set = lax.all_to_all(outgoing, "dp", split_axis=2, concat_axis=2, tiled=True)
    merged = jnp.sum(
        panel_set[:, None, :, :].astype(jnp.float32) * my_coef[None, :, :, None], axis=2
    ).astype(jnp.bfloat16)
    hidden_seg = hidden_act.reshape(seg_count, seg_len, ff_local)
    partial_rows = jnp.einsum(
        "stf,fsd->std", hidden_seg, merged, preferred_element_type=jnp.float32
    ).reshape(row_count, width)
    layer_out = lax.psum_scatter(
        partial_rows.astype(jnp.bfloat16), "tensor", scatter_dimension=1, tiled=True
    )
    full_cot = lax.all_gather(cotangent, "tensor", axis=1, tiled=True)
    cot_seg = full_cot.reshape(seg_count, seg_len, width)
    grad_hidden = (
        jnp.einsum("std,fsd->stf", cot_seg, merged, preferred_element_type=jnp.float32)
        .astype(jnp.bfloat16)
        .reshape(row_count, ff_local)
    )
    seg_grads = jnp.einsum(
        "stf,std->fsd", hidden_seg, cot_seg, preferred_element_type=jnp.float32
    ).astype(jnp.bfloat16)
    returned = lax.all_to_all(seg_grads, "dp", split_axis=2, concat_axis=2, tiled=True).reshape(
        ff_local, seg_count, dp_count, stripe
    )
    pool_coef = jax.vmap(merge_coefficients)(ids_by_dev, weights_by_dev, pools_all)
    coef_view = jnp.transpose(pool_coef, (1, 2, 0))
    group_sums = jnp.sum(
        returned[:, :, None, :, :].astype(jnp.float32) * coef_view[None, :, :, :, None], axis=1
    ).astype(jnp.bfloat16)
    grad_stripes = jnp.einsum(
        "fprd,pre->fed", group_sums, member_table, preferred_element_type=jnp.float32
    )
    slotted = (
        jnp.zeros((ff_local, slot_local * dp_count, stripe), jnp.float32)
        .at[:, owner_slot, :]
        .set(grad_stripes)
    )
    expert_grad = lax.all_to_all(
        slotted.astype(jnp.bfloat16), "dp", split_axis=1, concat_axis=2, tiled=True
    ).astype(slotted.dtype)
    return (layer_out, grad_hidden, expert_grad)


def solution(mesh):
    placed = (
        P("dp", "tensor"),
        P("dp", "tensor"),
        P("tensor", "dp", None),
        P("dp", None),
        P("dp", None),
        P(),
    )
    return jax.shard_map(
        body,
        mesh=mesh,
        in_specs=placed,
        out_specs=(P("dp", "tensor"), P("dp", "tensor"), P("tensor", "dp", None)),
        check_vma=False,
    )
```

profile of v0, /device:TPU:1, one launch (start us, length us, event | category | flops | bytes accessed | tf_op | source)
XLA Modules:
  0.0 478.6 jit_solution(9711148216334973201)
XLA Ops:
  7.2 4.5 copy.81
  11.7 0.5 broadcast.42
  12.2 11.6 %reduce.2 = bf16[2048,176]{1,0:T(8,128)(2,1)S(1)} reduce(bf16[2048,1,176]{2,1,0:T(2,128)(2,1)S(1)} %bitcast.55, bf16[]{:T(256)} %broadcast.42), dimensions={1}, to_apply=%bitcast.44.reduce_sub_computation | reduce | bytes 1441794
  23.9 0.0 copy-start.4
  23.9 0.0 copy-start.6
  23.9 2.6 reshape.124
  26.5 11.6 %all-to-all-start = ((bf16[64,2,2816]{2,1,0:T(2,128)(2,1)}), bf16[64,2,2816]{2,1,0:T(2,128)(2,1)S(1)}, u32[]{:S(2)}, u32[]{:S(2)}) async-start(bf16[64,2,2816]{2,1,0:T(2,128)(2,1)} %reshape.124), calls=%async_computation | async-start | bytes 1441792 | tf_op jit(solution)/shard_map/all_to_all | solution.py:44
  38.1 0.0 copy-done.4
  38.1 50.6 %all-gather = s32[64,2,4]{2,1,0:T(2,128)S(1)} all-gather(s32[1,2,4]{2,1,0:T(2,128)S(1)} %bitcast.65), channel_id=1, replica_groups=mesh['dp'=64,'tensor'=8] {'dp'}, dimensions={0}, use_global_device_ids=true | all-gather | bytes 2080 | tf_op jit(solution)/shard_map/all_gather | solution.py:35
  88.8 0.1 copy.78
  88.8 0.1 fusion.13
  88.9 0.1 copy.79
  89.0 0.2 reduce_window_sum.11
  89.2 0.1 copy.80
  89.3 0.1 reshape.96
  89.4 0.1 broadcast_in_dim.85
  89.5 0.2 broadcast_in_dim.86
  89.7 0.0 copy-done.6
  89.8 0.0 all-to-all-done
  89.8 3.2 reshape.125
  92.9 0.2 copy.95
  93.1 0.6 gather_fusion
  93.7 0.1 select_bitcast_fusion
  93.8 13.3 %gather_fusion.1 = bf16[384,176,32]{1,2,0:T(8,128)(2,1)} fusion(bf16[176,32,32]{0,2,1:T(8,128)(2,1)S(1)} %select_bitcast_fusion, s32[1024]{0:T(1024)S(1)} %pad_clamp_fusion), kind=kCustom, calls=%fused_computation.1 | custom fusion | bytes 8652288 | tf_op jit(solution)/shard_map/jit(_take)/gather | solution.py:46
  107.2 6.2 %broadcast_select_fusion = bf16[176,6,2048]{0,2,1:T(8,128)(2,1)S(1)} fusion(bf16[176,6,2048]{0,2,1:T(8,128)(2,1)} %bitcast.51, pred[6,2048]{1,0:T(8,128)(4,1)S(1)} %broadcast_in_dim.86), kind=kLoop, calls=%fused_computation.7 | loop fusion | flops 2162688 | bytes 8663040 | tf_op jit(solution)/shard_map/jit(_take)/select_n | solution.py:46
  113.4 22.3 %copy.82 = bf16[176,6,2048]{0,1,2:T(8,128)(2,1)} copy(bf16[176,6,2048]{0,2,1:T(8,128)(2,1)S(1)} %broadcast_select_fusion) | data formatting | bytes 8650752 | tf_op jit(solution)/shard_map/jit(_take)/select_n | solution.py:46
  135.7 8.6 %all-to-all-start.1 = ((bf16[176,6,2048]{0,1,2:T(8,128)(2,1)}), bf16[176,6,2048]{0,1,2:T(8,128)(2,1)}, u32[]{:S(2)}, u32[]{:S(2)}) async-start(bf16[176,6,2048]{0,1,2:T(8,128)(2,1)} %copy.82), calls=%async_computation.1 | async-start | bytes 16777216 | tf_op jit(solution)/shard_map/all_to_all | solution.py:47
  144.3 0.0 all-gather.4.cloned.1.call-start
  144.4 0.7 all-gather.4.cloned.1.call-update
  145.1 53.0 %all-gather.4.cloned.1.call-done = bf16[512,2048]{1,0:T(8,128)(2,1)} async-done(((bf16[512,256]{1,0:T(8,128)(2,1)}), bf16[512,2048]{1,0:T(8,128)(2,1)}) %all-gather.4.cloned.1.call-update) | async-done | bytes 2097168 | tf_op jit(solution)/shard_map/all_gather | solution.py:58
  198.0 0.0 copy-done.3
  198.0 2.1 fusion.2
  200.2 3.8 copy.87
  204.0 0.0 copy-start.5
  204.0 122.7 %all-to-all-done.1 = bf16[176,6,2048]{0,1,2:T(8,128)(2,1)} async-done(((bf16[176,6,2048]{0,1,2:T(8,128)(2,1)}), bf16[176,6,2048]{0,1,2:T(8,128)(2,1)}, u32[]{:S(2)}, u32[]{:S(2)}) %all-to-all-start.1) | async-done | bytes 4325408 | tf_op jit(solution)/shard_map/all_to_all | solution.py:47
  326.7 10.1 %all-to-all-start.2 = ((bf16[176,2,2048]{0,1,2:T(2,128)(2,1)}), bf16[176,2,2048]{0,1,2:T(2,128)(2,1)S(1)}, u32[]{:S(2)}, u32[]{:S(2)}) async-start(bf16[176,2,2048]{0,1,2:T(2,128)(2,1)} %copy.87), calls=%async_computation.3 | async-start | bytes 4194304 | tf_op jit(solution)/shard_map/all_to_all | solution.py:68
  336.8 0.0 reduce-scatter.2.cloned.1.call-start
  336.8 0.2 dynamic-slice_reduce_fusion
  337.0 0.0 copy-done.5
  337.0 0.1 select_reduce_fusion.2
  337.1 11.3 %copy.83 = bf16[176,6,2048]{2,0,1:T(8,128)(2,1)} copy(bf16[176,6,2048]{0,1,2:T(8,128)(2,1)} %all-to-all-done.1) | data formatting | bytes 8650752 | tf_op jit(solution)/shard_map/all_to_all | solution.py:47
  348.4 6.6 %convert_element_type.68 = f32[176,6,2048]{2,0,1:T(8,128)} convert(bf16[176,6,2048]{2,0,1:T(8,128)(2,1)} %copy.83) | non-fusion elementwise | flops 2162688 | bytes 12976128 | tf_op jit(solution)/shard_map/convert_element_type | solution.py:49
  355.0 4.8 multiply_reduce_fusion.1
  359.8 0.0 copy-start
  359.8 1.1 copy-done
  360.9 2.1 convolution_convert_fusion
  363.0 0.0 reduce-scatter.2.cloned.1.call-update
  363.0 53.9 %all-gather.1 = f32[64,2,4]{2,1,0:T(2,128)S(1)} all-gather(f32[1,2,4]{2,1,0:T(2,128)S(1)} %bitcast.66), channel_id=1, replica_groups=mesh['dp'=64,'tensor'=8] {'dp'}, dimensions={0}, use_global_device_ids=true | all-gather | bytes 2080 | tf_op jit(solution)/shard_map/all_gather | solution.py:36
  416.9 0.1 copy.90
  417.0 0.0 all-to-all-done.2
  417.0 0.6 bitcast_convert_fusion.1
  417.7 4.2 multiply_reduce_fusion
  421.9 3.7 fusion.3
  425.6 0.6 copy.92
  426.2 0.2 broadcast_in_dim.95
  426.4 1.6 scatter_fusion
  428.0 0.2 convert_element_type.80
  428.2 35.5 %all_to_all.31 = bf16[176,64,32]{0,2,1:T(8,128)(2,1)S(1)} all-to-all(bf16[176,64,32]{0,2,1:T(8,128)(2,1)S(1)} %convert_element_type.80), channel_id=1, replica_groups=mesh['dp'=64,'tensor'=8] {'dp'}, dimensions={1} | all-to-all | bytes 1441792 | tf_op jit(solution)/shard_map/all_to_all | solution.py:84
  463.7 1.5 bitcast_convert_fusion
  465.2 5.1 %copy.93 = f32[176,1,2048]{2,1,0:T(1,128)} copy(f32[176,1,2048]{0,2,1:T(8,128)} %bitcast_convert_fusion) | data formatting | bytes 2883584
  470.2 0.0 copy-done.1
  470.2 0.0 copy-done.2
  470.2 0.8 fusion.6
  471.1 0.7 copy.97
  (14 shorter events, 0.1 us)
Async XLA Ops:
  23.9 14.3 %copy-start.4 = (s32[2,4]{1,0:T(2,128)S(1)}, s32[2,4]{1,0:T(2,128)}, u32[]{:S(2)}) copy-start(s32[2,4]{1,0:T(2,128)} %param.9) | copy-start | bytes 100
  23.9 65.9 %copy-start.6 = (s32[32]{0:T(128)S(1)}, s32[32]{0:T(128)}, u32[]{:S(2)}) copy-start(s32[32]{0:T(128)} %param.11) | copy-start | bytes 388
  26.5 63.3 %all-to-all-start = ((bf16[64,2,2816]{2,1,0:T(2,128)(2,1)}), bf16[64,2,2816]{2,1,0:T(2,128)(2,1)S(1)}, u32[]{:S(2)}, u32[]{:S(2)}) async-start(bf16[64,2,2816]{2,1,0:T(2,128)(2,1)} %reshape.124), calls=%async_computation | async-start | bytes 1441792 | tf_op jit(solution)/shard_map/all_to_all | solution.py:44
  135.7 62.3 %copy-start.3 = (bf16[512,176]{0,1:T(8,128)(2,1)S(1)}, bf16[512,176]{0,1:T(8,128)(2,1)}, u32[]{:S(2)}) copy-start(bf16[512,176]{0,1:T(8,128)(2,1)} %param.6) | copy-start | bytes 540676
  135.7 191.0 %all-to-all-start.1 = ((bf16[176,6,2048]{0,1,2:T(8,128)(2,1)}), bf16[176,6,2048]{0,1,2:T(8,128)(2,1)}, u32[]{:S(2)}, u32[]{:S(2)}) async-start(bf16[176,6,2048]{0,1,2:T(8,128)(2,1)} %copy.82), calls=%async_computation.1 | async-start | bytes 16777216 | tf_op jit(solution)/shard_map/all_to_all | solution.py:47
  144.3 53.7 %all-gather.4.cloned.1.call-start = ((), (), s32[]{:S(2)}) async-start(), calls=%async_computation.6 | async-start | bytes 2359296 | tf_op jit(solution)/shard_map/all_gather | solution.py:58
  204.0 133.0 %copy-start.5 = (f32[2,4]{1,0:T(2,128)S(1)}, f32[2,4]{1,0:T(2,128)}, u32[]{:S(2)}) copy-start(f32[2,4]{1,0:T(2,128)} %param.10) | copy-start | bytes 100
  326.7 90.3 %all-to-all-start.2 = ((bf16[176,2,2048]{0,1,2:T(2,128)(2,1)}), bf16[176,2,2048]{0,1,2:T(2,128)(2,1)S(1)}, u32[]{:S(2)}, u32[]{:S(2)}) async-start(bf16[176,2,2048]{0,1,2:T(2,128)(2,1)} %copy.87), calls=%async_computation.3 | async-start | bytes 4194304 | tf_op jit(solution)/shard_map/all_to_all | solution.py:68
  336.8 135.0 %reduce-scatter.2.cloned.1.call-start = ((), (), s32[]{:S(2)}) async-start(), calls=%async_computation.5 | async-start | bytes 2359296 | tf_op jit(solution)/shard_map/reduce_scatter | solution.py:55
  359.8 1.1 copy-start
  465.2 5.1 %copy-start.1 = (bf16[176,2,2048]{2,0,1:T(8,128)(2,1)S(1)}, bf16[176,2,2048]{2,0,1:T(8,128)(2,1)}, u32[]{:S(2)}) copy-start(bf16[176,2,2048]{2,0,1:T(8,128)(2,1)} %copy-done) | copy-start | bytes 4325380
  465.2 5.1 %copy-start.2 = (bf16[512,2048]{1,0:T(8,128)(2,1)S(1)}, bf16[512,2048]{1,0:T(8,128)(2,1)}, u32[]{:S(2)}) copy-start(bf16[512,2048]{1,0:T(8,128)(2,1)} %all-gather.4.cloned.1.call-done) | copy-start | bytes 6291460
Sparse Core Ops, SparseCore 0:
  147.2 50.8 all-gather.3
  363.1 45.3 reduce-scatter.1
where the time goes:
time: 480 us; the launch traced here: 479 us
  waiting for transfers between devices  176 us (37%)
  blocking collectives  140 us (29%)
  local copies, waits for them, and re-layouts  72.6 us (15%)
  other arithmetic  36.2 us (8%)
  starting transfers between devices  30.4 us (6%)
  between operations  14.3 us (3%)
  matrix products  8.77 us (2%)
    all_to_all x1, waiting for transfers between devices, body(): lax.all_to_all(outgoing, 'dp', split_axis=2, concat_axis=2, tiled=True)  123 us
    all_gather x1, blocking collectives, body(): lax.all_gather(merge_weights, 'dp', axis=0, tiled=True)  53.9 us
    all_gather x1, waiting for transfers between devices, body(): full_cot = lax.all_gather(cotangent, 'tensor', axis=1, tiled=True)  53 us
    all_gather x1, blocking collectives, body(): lax.all_gather(expert_ids, 'dp', axis=0, tiled=True)  50.6 us
    all_to_all x1, blocking collectives, body(): lax.all_to_all(slotted.astype(jnp.bfloat16), 'dp', split_axis=1, concat_a...  35.5 us
    select_n x1, local copies, waits for them, and re-layouts, body(): jnp.take(by_expert, pools_all.T, axis=1).reshape(ff_local, POOL, width)  22.3 us
    unnamed x20, local copies, waits for them, and re-layouts  17.2 us
    gather x1, local copies, waits for them, and re-layouts, body(): jnp.take(by_expert, pools_all.T, axis=1).reshape(ff_local, POOL, width)  13.3 us
  transfers between devices with their start and end apart: 5, of which 2 were waited for; matrix products, arithmetic and copies ran while one was open for 11% of the time, Pallas kernels for 0%

commit v1 on v0

--- a/solution.py
+++ b/solution.py
@@ -6,6 +6,12 @@
 E = 32
 K = 4
 POOL = 6
+
+
+def gather_by_exchange(x, axis, dim):
+    size = lax.axis_size(axis)
+    repeats = [size if d == dim else 1 for d in range(x.ndim)]
+    return lax.all_to_all(jnp.tile(x, repeats), axis, split_axis=dim, concat_axis=dim, tiled=True)
 
 
 def pool_members(id_rows):
@@ -32,7 +38,7 @@
     seg_len = row_count // seg_count
     every_expert = jnp.arange(E, dtype=jnp.int32)
     all_ids, all_weights = (
-        lax.all_gather(expert_ids, "dp", axis=0, tiled=True),
+        gather_by_exchange(expert_ids, "dp", 0),
         lax.all_gather(merge_weights, "dp", axis=0, tiled=True),
     )
     ids_by_dev = all_ids.reshape(dp_count, seg_count, K)

time: 480 us -> 459 us (0.956)
  blocking collectives: 140 us -> 89.4 us
  waiting for transfers between devices: 176 us -> 197 us
  starting transfers between devices: 30.4 us -> 38.4 us
    all_gather x1 -> x0, blocking collectives: 50.6 us -> none  [body(): lax.all_gather(expert_ids, 'dp', axis=0, tiled=True)]
    all_to_all x1, waiting for transfers between devices: 0.01 us -> 20.6 us  [body(): lax.all_to_all(down_table, 'dp', split_axis=2, concat_axis=1, tiled=True)]
    all_to_all x0 -> x1, starting transfers between devices: none -> 11.6 us  [gather_by_exchange(): lax.all_to_all(jnp.tile(x, repeats), axis, split_axis=dim, concat_axis=di...]
  transfers between devices with their start and end apart: 5 -> 6, of which waited for: 2 -> 3; matrix products, arithmetic and copies ran while one was open for 11% -> 15% of each run, Pallas kernels for 0% -> 0%
where the time goes in v1:
time: 459 us; the launch traced here: 458 us
  waiting for transfers between devices  197 us (43%)
  blocking collectives  89.4 us (19%)
  local copies, waits for them, and re-layouts  73.9 us (16%)
  starting transfers between devices  38.4 us (8%)
  other arithmetic  36.2 us (8%)
  between operations  14.3 us (3%)
  matrix products  8.77 us (2%)
    all_to_all x1, waiting for transfers between devices, body(): lax.all_to_all(outgoing, 'dp', split_axis=2, concat_axis=2, tiled=True)  123 us
    all_gather x1, blocking collectives, body(): lax.all_gather(merge_weights, 'dp', axis=0, tiled=True)  53.9 us
    all_gather x1, waiting for transfers between devices, body(): full_cot = lax.all_gather(cotangent, 'tensor', axis=1, tiled=True)  53 us
    all_to_all x1, blocking collectives, body(): lax.all_to_all(slotted.astype(jnp.bfloat16), 'dp', split_axis=1, concat_a...  35.5 us
    select_n x1, local copies, waits for them, and re-layouts, body(): jnp.take(by_expert, pools_all.T, axis=1).reshape(ff_local, POOL, width)  22.3 us
    all_to_all x1, waiting for transfers between devices, body(): lax.all_to_all(down_table, 'dp', split_axis=2, concat_axis=1, tiled=True)  20.6 us
    unnamed x20, local copies, waits for them, and re-layouts  17.2 us
    gather x1, local copies, waits for them, and re-layouts, body(): jnp.take(by_expert, pools_all.T, axis=1).reshape(ff_local, POOL, width)  13.3 us
  transfers between devices with their start and end apart: 6, of which 3 were waited for; matrix products, arithmetic and copies ran while one was open for 15% of the time, Pallas kernels for 0%

profile of v1, /device:TPU:1, one launch (start us, length us, event | category | flops | bytes accessed | tf_op | source)
XLA Modules:
  0.0 457.9 jit_solution(16521613362879931998)
XLA Ops:
  7.2 1.3 tile.2
  8.5 11.6 %all-to-all-start = ((s32[64,2,4]{2,1,0:T(2,128)}), s32[64,2,4]{2,1,0:T(2,128)S(1)}, u32[]{:S(2)}, u32[]{:S(2)}) async-start(s32[64,2,4]{2,1,0:T(2,128)} %tile.2), calls=%async_computation | async-start | bytes 131072 | tf_op jit(solution)/shard_map/all_to_all | solution.py:14
  20.1 4.5 copy.81
  24.7 0.5 broadcast.45
  25.2 11.6 %reduce.2 = bf16[2048,176]{1,0:T(8,128)(2,1)S(1)} reduce(bf16[2048,1,176]{2,1,0:T(2,128)(2,1)S(1)} %bitcast.54, bf16[]{:T(256)} %broadcast.45), dimensions={1}, to_apply=%bitcast.43.reduce_sub_computation | reduce | bytes 1441794
  36.8 0.0 copy-start.6
  36.8 2.6 reshape.129
  39.4 0.0 all-to-all-done
  39.4 10.3 %all-to-all-start.1 = ((bf16[64,2,2816]{2,1,0:T(2,128)(2,1)}), bf16[64,2,2816]{2,1,0:T(2,128)(2,1)S(1)}, u32[]{:S(2)}, u32[]{:S(2)}) async-start(bf16[64,2,2816]{2,1,0:T(2,128)(2,1)} %reshape.129), calls=%async_computation.1 | async-start | bytes 1441792 | tf_op jit(solution)/shard_map/all_to_all | solution.py:50
  49.8 0.0 copy-done.6
  49.8 0.1 copy.78
  49.9 0.1 fusion.13
  50.0 0.1 copy.79
  50.0 0.2 reduce_window_sum.11
  50.3 0.1 copy.80
  50.4 0.1 reshape.105
  50.5 0.1 broadcast_in_dim.85
  50.6 0.2 broadcast_in_dim.86
  50.8 20.6 %all-to-all-done.1 = bf16[64,2,2816]{2,1,0:T(2,128)(2,1)S(1)} async-done(((bf16[64,2,2816]{2,1,0:T(2,128)(2,1)}), bf16[64,2,2816]{2,1,0:T(2,128)(2,1)S(1)}, u32[]{:S(2)}, u32[]{:S(2)}) %all-to-all-start.1) | async-done | bytes 720928 | tf_op jit(solution)/shard_map/all_to_all | solution.py:50
  71.3 3.1 reshape.130
  74.5 0.2 copy.95
  74.7 0.6 gather_fusion
  75.3 0.1 select_bitcast_fusion
  75.4 13.3 %gather_fusion.1 = bf16[384,176,32]{1,2,0:T(8,128)(2,1)} fusion(bf16[176,32,32]{0,2,1:T(8,128)(2,1)S(1)} %select_bitcast_fusion, s32[1024]{0:T(1024)S(1)} %pad_clamp_fusion), kind=kCustom, calls=%fused_computation.1 | custom fusion | bytes 8652288 | tf_op jit(solution)/shard_map/jit(_take)/gather | solution.py:52
  88.7 6.2 %broadcast_select_fusion = bf16[176,6,2048]{0,2,1:T(8,128)(2,1)S(1)} fusion(bf16[176,6,2048]{0,2,1:T(8,128)(2,1)} %bitcast.50, pred[6,2048]{1,0:T(8,128)(4,1)S(1)} %broadcast_in_dim.86), kind=kLoop, calls=%fused_computation.7 | loop fusion | flops 2162688 | bytes 8663040 | tf_op jit(solution)/shard_map/jit(_take)/select_n | solution.py:52
  94.9 22.3 %copy.82 = bf16[176,6,2048]{0,1,2:T(8,128)(2,1)} copy(bf16[176,6,2048]{0,2,1:T(8,128)(2,1)S(1)} %broadcast_select_fusion) | data formatting | bytes 8650752 | tf_op jit(solution)/shard_map/jit(_take)/select_n | solution.py:52
  117.2 6.3 %all-to-all-start.2 = ((bf16[176,6,2048]{0,1,2:T(8,128)(2,1)}), bf16[176,6,2048]{0,1,2:T(8,128)(2,1)}, u32[]{:S(2)}, u32[]{:S(2)}) async-start(bf16[176,6,2048]{0,1,2:T(8,128)(2,1)} %copy.82), calls=%async_computation.2 | async-start | bytes 16777216 | tf_op jit(solution)/shard_map/all_to_all | solution.py:53
  123.6 0.0 all-gather.3.cloned.1.call-start
  123.6 0.7 all-gather.3.cloned.1.call-update
  124.3 53.0 %all-gather.3.cloned.1.call-done = bf16[512,2048]{1,0:T(8,128)(2,1)} async-done(((bf16[512,256]{1,0:T(8,128)(2,1)}), bf16[512,2048]{1,0:T(8,128)(2,1)}) %all-gather.3.cloned.1.call-update) | async-done | bytes 2097168 | tf_op jit(solution)/shard_map/all_gather | solution.py:64
  177.3 0.0 copy-done.3
  177.3 2.1 fusion.2
  179.4 3.8 copy.87
  183.3 122.7 %all-to-all-done.2 = bf16[176,6,2048]{0,1,2:T(8,128)(2,1)} async-done(((bf16[176,6,2048]{0,1,2:T(8,128)(2,1)}), bf16[176,6,2048]{0,1,2:T(8,128)(2,1)}, u32[]{:S(2)}, u32[]{:S(2)}) %all-to-all-start.2) | async-done | bytes 4325408 | tf_op jit(solution)/shard_map/all_to_all | solution.py:53
  306.0 10.1 %all-to-all-start.3 = ((bf16[176,2,2048]{0,1,2:T(2,128)(2,1)}), bf16[176,2,2048]{0,1,2:T(2,128)(2,1)S(1)}, u32[]{:S(2)}, u32[]{:S(2)}) async-start(bf16[176,2,2048]{0,1,2:T(2,128)(2,1)} %copy.87), calls=%async_computation.4 | async-start | bytes 4194304 | tf_op jit(solution)/shard_map/all_to_all | solution.py:74
  316.0 0.0 reduce-scatter.2.cloned.1.call-start
  316.1 0.2 dynamic-slice_reduce_fusion
  316.3 0.0 copy-done.4
  316.3 0.0 copy-done.5
  316.3 0.1 select_reduce_fusion.2
  316.4 11.3 %copy.83 = bf16[176,6,2048]{2,0,1:T(8,128)(2,1)} copy(bf16[176,6,2048]{0,1,2:T(8,128)(2,1)} %all-to-all-done.2) | data formatting | bytes 8650752 | tf_op jit(solution)/shard_map/all_to_all | solution.py:53
  327.7 6.6 %convert_element_type.68 = f32[176,6,2048]{2,0,1:T(8,128)} convert(bf16[176,6,2048]{2,0,1:T(8,128)(2,1)} %copy.83) | non-fusion elementwise | flops 2162688 | bytes 12976128 | tf_op jit(solution)/shard_map/convert_element_type | solution.py:55
  334.3 4.8 %multiply_reduce_fusion.1 = bf16[176,2,2048]{2,0,1:T(8,128)(2,1)S(1)} fusion(f32[2,6]{1,0:T(2,128)S(1)} %select_reduce_fusion.2, f32[176,6,2048]{2,0,1:T(8,128)} %convert_element_type.68), kind=kLoop, calls=%fused_computation.4 | loop fusion | flops 7929856 | bytes 10092592 | tf_op jit(solution)/shard_map/reduce_sum | solution.py:54
  339.1 0.0 copy-start
  339.1 1.1 copy-done
  340.2 2.1 convolution_convert_fusion
  342.3 0.0 reduce-scatter.2.cloned.1.call-update
  342.3 53.9 %all-gather = f32[64,2,4]{2,1,0:T(2,128)S(1)} all-gather(f32[1,2,4]{2,1,0:T(2,128)S(1)} %bitcast.64), channel_id=1, replica_groups=mesh['dp'=64,'tensor'=8] {'dp'}, dimensions={0}, use_global_device_ids=true | all-gather | bytes 2080 | tf_op jit(solution)/shard_map/all_gather | solution.py:42
  396.2 0.1 copy.90
  396.3 0.0 all-to-all-done.3
  396.3 0.6 bitcast_convert_fusion.1
  396.9 4.2 multiply_reduce_fusion
  401.2 3.7 fusion.3
  404.8 0.6 copy.92
  405.5 0.2 broadcast_in_dim.95
  405.7 1.6 scatter_fusion
  407.3 0.2 convert_element_type.80
  407.5 35.5 %all_to_all.37 = bf16[176,64,32]{0,2,1:T(8,128)(2,1)S(1)} all-to-all(bf16[176,64,32]{0,2,1:T(8,128)(2,1)S(1)} %convert_element_type.80), channel_id=1, replica_groups=mesh['dp'=64,'tensor'=8] {'dp'}, dimensions={1} | all-to-all | bytes 1441792 | tf_op jit(solution)/shard_map/all_to_all | solution.py:90
  443.0 1.5 bitcast_convert_fusion
  444.4 5.1 %copy.93 = f32[176,1,2048]{2,1,0:T(1,128)} copy(f32[176,1,2048]{0,2,1:T(8,128)} %bitcast_convert_fusion) | data formatting | bytes 2883584
  449.5 0.0 copy-done.1
  449.5 0.0 copy-done.2
  449.5 0.8 fusion.6
  450.4 0.7 copy.97
  (16 shorter events, 0.1 us)
Async XLA Ops:
  8.5 30.9 %all-to-all-start = ((s32[64,2,4]{2,1,0:T(2,128)}), s32[64,2,4]{2,1,0:T(2,128)S(1)}, u32[]{:S(2)}, u32[]{:S(2)}) async-start(s32[64,2,4]{2,1,0:T(2,128)} %tile.2), calls=%async_computation | async-start | bytes 131072 | tf_op jit(solution)/shard_map/all_to_all | solution.py:14
  36.8 12.9 %copy-start.6 = (s32[32]{0:T(128)S(1)}, s32[32]{0:T(128)}, u32[]{:S(2)}) copy-start(s32[32]{0:T(128)} %param.11) | copy-start | bytes 388
  39.4 31.9 %all-to-all-start.1 = ((bf16[64,2,2816]{2,1,0:T(2,128)(2,1)}), bf16[64,2,2816]{2,1,0:T(2,128)(2,1)S(1)}, u32[]{:S(2)}, u32[]{:S(2)}) async-start(bf16[64,2,2816]{2,1,0:T(2,128)(2,1)} %reshape.129), calls=%async_computation.1 | async-start | bytes 1441792 | tf_op jit(solution)/shard_map/all_to_all | solution.py:50
  117.2 60.0 %copy-start.3 = (bf16[512,176]{0,1:T(8,128)(2,1)S(1)}, bf16[512,176]{0,1:T(8,128)(2,1)}, u32[]{:S(2)}) copy-start(bf16[512,176]{0,1:T(8,128)(2,1)} %param.6) | copy-start | bytes 540676
  117.2 188.7 %all-to-all-start.2 = ((bf16[176,6,2048]{0,1,2:T(8,128)(2,1)}), bf16[176,6,2048]{0,1,2:T(8,128)(2,1)}, u32[]{:S(2)}, u32[]{:S(2)}) async-start(bf16[176,6,2048]{0,1,2:T(8,128)(2,1)} %copy.82), calls=%async_computation.2 | async-start | bytes 16777216 | tf_op jit(solution)/shard_map/all_to_all | solution.py:53
  123.6 53.7 %all-gather.3.cloned.1.call-start = ((), (), s32[]{:S(2)}) async-start(), calls=%async_computation.7 | async-start | bytes 2359296 | tf_op jit(solution)/shard_map/all_gather | solution.py:64
  183.3 133.0 %copy-start.4 = (s32[2,4]{1,0:T(2,128)S(1)}, s32[2,4]{1,0:T(2,128)}, u32[]{:S(2)}) copy-start(s32[2,4]{1,0:T(2,128)} %param.9) | copy-start | bytes 100
  183.3 133.0 %copy-start.5 = (f32[2,4]{1,0:T(2,128)S(1)}, f32[2,4]{1,0:T(2,128)}, u32[]{:S(2)}) copy-start(f32[2,4]{1,0:T(2,128)} %param.10) | copy-start | bytes 100
  306.0 90.3 %all-to-all-start.3 = ((bf16[176,2,2048]{0,1,2:T(2,128)(2,1)}), bf16[176,2,2048]{0,1,2:T(2,128)(2,1)S(1)}, u32[]{:S(2)}, u32[]{:S(2)}) async-start(bf16[176,2,2048]{0,1,2:T(2,128)(2,1)} %copy.87), calls=%async_computation.4 | async-start | bytes 4194304 | tf_op jit(solution)/shard_map/all_to_all | solution.py:74
  316.0 135.0 %reduce-scatter.2.cloned.1.call-start = ((), (), s32[]{:S(2)}) async-start(), calls=%async_computation.6 | async-start | bytes 2359296 | tf_op jit(solution)/shard_map/reduce_scatter | solution.py:61
  339.1 1.1 copy-start
  444.4 5.1 %copy-start.1 = (bf16[176,2,2048]{2,0,1:T(8,128)(2,1)S(1)}, bf16[176,2,2048]{2,0,1:T(8,128)(2,1)}, u32[]{:S(2)}) copy-start(bf16[176,2,2048]{2,0,1:T(8,128)(2,1)} %copy-done) | copy-start | bytes 4325380
  444.4 5.1 %copy-start.2 = (bf16[512,2048]{1,0:T(8,128)(2,1)S(1)}, bf16[512,2048]{1,0:T(8,128)(2,1)}, u32[]{:S(2)}) copy-start(bf16[512,2048]{1,0:T(8,128)(2,1)} %all-gather.3.cloned.1.call-done) | copy-start | bytes 6291460
Sparse Core Ops, SparseCore 0:
  126.4 50.8 all-gather.2
  342.4 45.3 reduce-scatter.1
